TPU v7x, 32 devices: a whole 2x2x4 slice. The times are simulated.
32 devices in a mesh: space: 4 (over x, core), mem: 8 (over z, y).
Axes of the slice: x: 2, y: 2, z: 4, core: 2. Of those that a mesh axis runs over, the one named last changes fastest.
Arguments:
- prior_ensemble: float32 [512, 8192], P('mem', 'space'), may hold values from -5 to 5
- terminal_particles: float32 [512, 8192], P(None, ('space', 'mem')), may hold values from -5 to 5
- reverse_perturbation: float32 [3, 512, 8192], P(None, None, ('space', 'mem')), may hold values from -6 to 6
- measured_angles: float32 [8192], P(('space', 'mem')), may hold values from -1.3 to 1.3
Outputs:
- analysis: float32 [512, 8192], P(None, ('space', 'mem'))
All inputs are finite; a program needn't handle non-finite values.
Results may differ from a plain program's by a relative error of at most 0.0003.
Values sent between devices are 32-bit elements; how exact they have to be, the bound alone decides.
A program may use at most 64 MiB of HBM per device.

v0:
```python
import math

import jax
import jax.numpy as jnp
from jax import lax
from jax.sharding import PartitionSpec as P

ITERS = 3


def member_weights(inner_pairing_matrix, particle_lengths, alpha, sigma2, temper):
    logits = (2.0 * alpha * inner_pairing_matrix - alpha * alpha * particle_lengths[None, :]) / (
        2.0 * sigma2 * temper
    )
    return jax.nn.softmax(logits, axis=1)


def per_device(prior_ensemble, terminal_particles, reverse_perturbation, measured_angles):
    peak_log_likelihood = lax.Precision.HIGHEST
    particle_vectors = lax.all_to_all(
        prior_ensemble, "mem", split_axis=1, concat_axis=0, tiled=True
    )
    devices_all = lax.axis_size("space") * lax.axis_size("mem")
    temper = math.sqrt(particle_vectors.shape[1] * devices_all)
    local_norms = jnp.sum(prior_ensemble * prior_ensemble, axis=1)
    summed = lax.psum(local_norms, "space")
    particle_lengths = lax.all_gather(summed, "mem", axis=0, tiled=True)
    gaussian_variates = terminal_particles
    for step in range(ITERS):
        t = 1.0 - step / ITERS
        dt = 1.0 / ITERS
        alpha = 1.0 - 0.5 * t
        drift = -0.5 / alpha
        g2 = 1.0 + t / alpha
        damp = 1.0 - t
        partial_gram = jnp.einsum(
            "sv,mv->sm",
            gaussian_variates,
            particle_vectors,
            precision=peak_log_likelihood,
            preferred_element_type=jnp.float32,
        )
        inner_pairing_matrix = lax.psum(partial_gram, ("space", "mem"))
        annealed_importance = member_weights(
            inner_pairing_matrix, particle_lengths, alpha, t, temper
        )
        mixed_correction = jnp.dot(
            annealed_importance,
            particle_vectors,
            precision=peak_log_likelihood,
            preferred_element_type=jnp.float32,
        )
        score = -(gaussian_variates - alpha * mixed_correction) / t + damp * 4.0 * (
            measured_angles[None, :] - jnp.arctan(gaussian_variates)
        ) / (1.0 + gaussian_variates * gaussian_variates)
        gaussian_variates = (
            gaussian_variates
            + dt * (-drift * gaussian_variates + g2 * score)
            + math.sqrt(dt * g2) * reverse_perturbation[step]
        )
    return gaussian_variates


def solution(mesh):
    in_specs = (
        P("mem", "space"),
        P(None, ("space", "mem")),
        P(None, None, ("space", "mem")),
        P(("space", "mem")),
    )
    out_specs = P(None, ("space", "mem"))
    return jax.shard_map(
        per_device, mesh=mesh, in_specs=in_specs, out_specs=out_specs, check_vma=False
    )
```

profile of v0, /device:TPU:0, one launch (start us, length us, event | category | flops | bytes accessed | tf_op | source)
XLA Modules:
  0.0 456.9 jit_solution(2915807042031662705)
XLA Ops:
  6.5 0.0 copy-start.4
  6.5 0.0 all-reduce.5.cloned.1.call-start
  6.5 1.1 copy.8
  7.7 21.6 %all_to_all.19 = f32[64,8,256]{2,0,1:T(8,128)S(1)} all-to-all(f32[64,8,256]{2,0,1:T(8,128)S(1)} %bitcast.29), channel_id=1, replica_groups=mesh['space'=4,'mem'=8] {'mem'}, dimensions={1} | all-to-all | bytes 1048576 | tf_op jit(solution)/shard_map/all_to_all | solution.py:20
  29.3 0.0 copy-start
  29.3 0.0 copy-done.4
  29.3 0.0 copy-start.8
  29.3 0.0 copy-start.3
  29.3 2.1 fusion.1
  31.4 0.0 all-reduce.5.cloned.1.call-update
  31.4 0.0 copy-done
  31.4 0.0 all-reduce.7.cloned.1.call-start
  31.5 0.0 copy-done.8
  31.5 0.6 dynamic-slice
  32.7 0.0 copy-done.3
  32.7 0.1 multiply_reduce_fusion
  32.9 5.7 %psum.29 = f32[64]{0:T(128)S(1)} all-reduce(f32[64]{0:T(128)S(1)} %multiply_reduce_fusion), channel_id=1, replica_groups=mesh['space'=4,'mem'=8] {'space'}, use_global_device_ids=true, to_apply=%region_2.0 | all-reduce | flops 64 | bytes 512 | tf_op jit(solution)/shard_map/psum | solution.py:26
  38.5 0.2 dynamic-update-slice
  38.8 20.0 %all-reduce = f32[512]{0:T(512)S(1)} all-reduce(f32[512]{0:T(512)S(1)} %dynamic-update-slice), channel_id=1, replica_groups=mesh['space'=4,'mem'=8] {'mem'}, use_global_device_ids=true, to_apply=%add | all-reduce | flops 512 | bytes 4096
  58.8 102.5 %all-reduce.5.cloned.1.call-done = f32[512,512]{1,0:T(8,128)} async-done(((f32[512,512]{1,0:T(8,128)}), f32[512,512]{1,0:T(8,128)}) %all-reduce.5.cloned.1.call-update) | async-done | bytes 1048592 | tf_op jit(solution)/shard_map/psum | solution.py:43
  161.3 0.0 copy-start.7
  161.3 2.4 subtract_multiply_fusion.2
  163.7 0.0 copy-start.1
  163.7 0.0 copy-start.6
  163.7 3.7 online-softmax
  167.4 0.0 copy-done.7
  167.4 0.0 copy-done.1
  167.4 0.0 copy-done.6
  167.4 3.9 fusion
  171.3 0.0 all-reduce.7.cloned.1.call-update
  171.3 0.2 all-reduce.9.cloned.1.call-start
  171.6 129.5 %all-reduce.7.cloned.1.call-done = f32[512,512]{1,0:T(8,128)} async-done(((f32[512,512]{1,0:T(8,128)}), f32[512,512]{1,0:T(8,128)}) %all-reduce.7.cloned.1.call-update) | async-done | bytes 1048592 | tf_op jit(solution)/shard_map/psum | solution.py:43
  301.1 2.4 subtract_multiply_fusion.1
  303.5 0.0 copy-start.5
  303.5 3.6 online-softmax.1
  307.1 0.0 copy-done.5
  307.1 0.0 copy-start.2
  307.1 2.8 bitcast_add_fusion.1
  309.9 0.0 copy-done.2
  309.9 2.1 fusion.2
  312.0 0.0 all-reduce.9.cloned.1.call-update
  312.0 129.8 %all-reduce.9.cloned.1.call-done = f32[512,512]{1,0:T(8,128)} async-done(((f32[512,512]{1,0:T(8,128)}), f32[512,512]{1,0:T(8,128)}) %all-reduce.9.cloned.1.call-update) | async-done | bytes 1048592 | tf_op jit(solution)/shard_map/psum | solution.py:43
  441.8 2.4 subtract_multiply_fusion
  444.2 3.6 online-softmax.2
  447.7 2.7 bitcast_add_fusion
  (2 shorter events, 0.0 us)
Async XLA Ops:
  6.5 22.8 %copy-start.4 = (f32[512,256]{1,0:T(8,128)S(1)}, f32[512,256]{1,0:T(8,128)}, u32[]{:S(2)}) copy-start(f32[512,256]{1,0:T(8,128)} %param.5) | copy-start | bytes 1572868
  6.5 154.7 %all-reduce.5.cloned.1.call-start = ((), (), s32[]{:S(2)}) async-start(), calls=%async_computation.1 | async-start | bytes 2097152 | tf_op jit(solution)/shard_map/psum | solution.py:43
  29.3 2.1 copy-start
  29.3 2.2 copy-start.8
  29.3 3.4 copy-start.3
  31.4 269.7 %all-reduce.7.cloned.1.call-start = ((), (), s32[]{:S(2)}) async-start(), calls=%async_computation.2 | async-start | bytes 2097152 | tf_op jit(solution)/shard_map/psum | solution.py:43
  161.3 6.1 %copy-start.7 = (f32[256]{0:T(256)S(1)}, f32[256]{0:T(256)}, u32[]{:S(2)}) copy-start(f32[256]{0:T(256)} %param.7) | copy-start | bytes 3076
  163.7 3.7 copy-start.1
  163.7 3.7 copy-start.6
  171.3 270.4 %all-reduce.9.cloned.1.call-start = ((), (), s32[]{:S(2)}) async-start(), calls=%async_computation.3 | async-start | bytes 2097152 | tf_op jit(solution)/shard_map/psum | solution.py:43
  303.5 3.6 copy-start.5
  307.1 2.8 copy-start.2
Sparse Core Ops, SparseCore 0:
  31.5 129.6 all-reduce.4
  171.5 129.5 all-reduce.6
  312.1 129.6 all-reduce.8
where the time goes:
time: 457 us
  waiting for transfers between devices  362 us (79%)
  blocking collectives  47.3 us (10%)
  between operations  13.8 us (3%)
  other arithmetic  12.8 us (3%)
  Pallas kernels  10.9 us (2%)
  matrix products  8.05 us (2%)
    psum x3, waiting for transfers between devices, per_device(): inner_pairing_matrix = lax.psum(partial_gram, ('space', 'mem'))  362 us
    all_to_all x1, blocking collectives, per_device(): lax.all_to_all(prior_ensemble, 'mem', split_axis=1, concat_axis=0, tiled=...  21.6 us
    unnamed x1, blocking collectives  20 us
    unnamed x3, Pallas kernels  10.9 us
  transfers between devices with their start and end apart: 3, of which 3 were waited for; matrix products, arithmetic and copies ran while one was open for 0% of the time, Pallas kernels for 0%

commit v1 on v0

v1 whole, which is shorter than its diff:
```python
import functools
import math

import jax
import jax.numpy as jnp
from jax import lax
from jax.experimental import pallas as pl
from jax.experimental.pallas import tpu as pltpu
from jax.sharding import PartitionSpec as P

ITERS = 3
CHUNKS = 2
CORES = 2
SUBLANES = 8
MESH = pl.DeviceIdType.MESH
HIGHEST = lax.Precision.HIGHEST


def dot(a, b, contract_b):
    return lax.dot_general(
        a,
        b,
        (((1,), (contract_b,)), ((), ())),
        precision=HIGHEST,
        preferred_element_type=jnp.float32,
    )


def arctan(x):
    a = jnp.abs(x)
    big = a > 2.414213562373095
    mid = a > 0.4142135623730950
    num = jnp.where(big, -1.0, jnp.where(mid, a - 1.0, a))
    den = jnp.where(big, a, jnp.where(mid, a + 1.0, 1.0))
    base = jnp.where(big, math.pi / 2, jnp.where(mid, math.pi / 4, 0.0))
    r = num / den
    s = r * r
    poly = ((8.05374449538e-2 * s - 1.38776856032e-1) * s + 1.99777106478e-1) * s
    poly = (poly - 3.33329491539e-1) * s * r + r
    y = base + poly
    return jnp.where(x < 0.0, -y, y)


def rows_at(start, size):
    return pl.ds(pl.multiple_of(start, SUBLANES), size)


def kernel(
    plan,
    prior,
    terminal,
    perturbation,
    angles,
    out,
    x,
    z,
    noise,
    give,
    keep,
    core_in,
    xy_in,
    part,
    z_in,
    w,
    send,
    recv,
    xsend,
    xrecv,
    local,
    osem,
):
    n_space, n_mem, ny, nz, scatter_z, temper = plan
    nxy = (n_space // CORES) * ny
    rows = z.shape[0] // CHUNKS
    rows2 = rows // CORES
    rows3 = rows2 // nxy
    rows4 = rows3 // nz if scatter_z else rows3
    members = prior.shape[0]
    variables = x.shape[1]

    sp = lax.axis_index("space")
    me = lax.axis_index("mem")
    core = lax.rem(sp, CORES)
    other = 1 - core
    xi = lax.div(sp, CORES)
    yi = lax.rem(me, ny)
    zi = lax.div(me, ny)
    q = xi * ny + yi

    core_dev = (xi * CORES + other, me)

    def xy_peer(d):
        p = lax.rem(q + d, nxy)
        return p, (lax.div(p, ny) * CORES + core, zi * ny + lax.rem(p, ny))

    def z_peer(d):
        p = lax.rem(zi + d, nz)
        return p, (sp, p * ny + yi)

    def mem_peer(d):
        p = lax.rem(me + d, n_mem)
        return p, (sp, p)

    def cols(p):
        return pl.ds(pl.multiple_of(p * variables, variables), variables)

    loads = [
        pltpu.make_async_copy(terminal, z, local.at[0]),
        pltpu.make_async_copy(perturbation, noise, local.at[1]),
        pltpu.make_async_copy(
            prior.at[:, cols(me)], x.at[rows_at(me * members, members), :], local.at[2]
        ),
    ]
    for copy in loads:
        copy.start()

    barrier = pltpu.get_barrier_semaphore()
    greet = [core_dev]
    greet += [xy_peer(d)[1] for d in range(1, nxy)]
    greet += [mem_peer(d)[1] for d in range(1, n_mem)]
    for dev in greet:
        pl.semaphore_signal(barrier, inc=1, device_id=dev, device_id_type=MESH)
    pl.semaphore_wait(barrier, len(greet))

    exchange = []
    for d in range(1, n_mem):
        p, dev = mem_peer(d)
        exchange.append(
            pltpu.make_async_remote_copy(
                src_ref=prior.at[:, cols(p)],
                dst_ref=x.at[rows_at(me * members, members), :],
                send_sem=xsend.at[d - 1],
                recv_sem=xrecv.at[d - 1],
                device_id=dev,
                device_id_type=MESH,
            )
        )
        exchange[-1].start()
    for copy in loads:
        copy.wait()
    for copy in exchange:
        copy.wait_recv()

    xs = x[...]
    norms = dot(jnp.ones((SUBLANES, variables), jnp.float32), xs * xs, 1)[:1]

    first_xy = 1
    first_z = first_xy + nxy - 1
    first_gz = first_z + nz - 1
    first_gxy = first_gz + nz - 1
    last_core = first_gxy + nxy - 1

    def chunk(c):
        base = c * rows
        for k in range(ITERS):
            t = 1.0 - k / ITERS
            dt = 1.0 / ITERS
            alpha = 1.0 - 0.5 * t
            drift = -0.5 / alpha
            g2 = 1.0 + t / alpha
            damp = 1.0 - t
            started = []

            def put(src, dst, i, dev):
                copy = pltpu.make_async_remote_copy(
                    src_ref=src,
                    dst_ref=dst,
                    send_sem=send.at[k % 2, c, i],
                    recv_sem=recv.at[k % 2, c, i],
                    device_id=dev,
                    device_id_type=MESH,
                )
                copy.start()
                started.append(copy)
                return copy

            def numerator(half):
                zs = z[rows_at(base + half * rows2, rows2), :]
                return 2.0 * alpha * dot(zs, x[...], 1) - alpha * alpha * norms

            give[c] = numerator(other)
            swap = put(give.at[c], core_in.at[c], 0, core_dev)
            keep[c] = numerator(core)
            yield
            swap.wait_recv()
            group = []
            for d in range(1, nxy):
                p, dev = xy_peer(d)
                block = rows_at(p * rows3, rows3)
                keep[c, block, :] = keep[c, block, :] + core_in[c, block, :]
                group.append(put(keep.at[c, block, :], xy_in.at[c, d - 1], first_xy + d - 1, dev))
            block = rows_at(q * rows3, rows3)
            total = keep[c, block, :] + core_in[c, block, :]
            yield
            for d, copy in enumerate(group):
                copy.wait_recv()
                total = total + xy_in[c, d]
            part[c] = total
            group = []
            for d in range(1, nz):
                p, dev = z_peer(d)
                src = part.at[c, rows_at(p * rows4, rows4), :] if scatter_z else part.at[c]
                group.append(put(src, z_in.at[k % 2, c, d - 1], first_z + d - 1, dev))
            total = part[c, rows_at(zi * rows4, rows4), :] if scatter_z else total
            yield
            for d, copy in enumerate(group):
                copy.wait_recv()
                total = total + z_in[k % 2, c, d]
            logits = total / (2.0 * t * temper)
            e = jnp.exp(logits - jnp.max(logits, axis=1, keepdims=True))
            weights = e / jnp.sum(e, axis=1, keepdims=True)
            mine = core * rows2 + q * rows3
            if scatter_z:
                block = rows_at(mine + zi * rows4, rows4)
                w[c, block, :] = weights
                group = [
                    put(w.at[c, block, :], w.at[c, block, :], first_gz + d - 1, z_peer(d)[1])
                    for d in range(1, nz)
                ]
                yield
                for copy in group:
                    copy.wait_recv()
            else:
                w[c, rows_at(mine, rows3), :] = weights
            block = rows_at(mine, rows3)
            group = [
                put(w.at[c, block, :], w.at[c, block, :], first_gxy + d - 1, xy_peer(d)[1])
                for d in range(1, nxy)
            ]
            yield
            for copy in group:
                copy.wait_recv()
            half = rows_at(core * rows2, rows2)
            swap = put(w.at[c, half, :], w.at[c, half, :], last_core, core_dev)

            def advance(half):
                where = rows_at(base + half * rows2, rows2)
                blend = dot(w[c, rows_at(half * rows2, rows2), :], x[...], 0)
                zs = z[where, :]
                score = -(zs - alpha * blend) / t + damp * 4.0 * (
                    angles[...] - arctan(zs)
                ) / (1.0 + zs * zs)
                z[where, :] = (
                    zs
                    + dt * (-drift * zs + g2 * score)
                    + math.sqrt(dt * g2) * noise[k, where, :]
                )

            advance(core)
            yield
            swap.wait_recv()
            advance(other)
            for copy in started:
                copy.wait_send()
        result = pltpu.make_async_copy(
            z.at[pl.ds(base, rows), :], out.at[pl.ds(base, rows), :], osem.at[c]
        )
        result.start()
        yield
        result.wait()

    running = [chunk(c) for c in range(CHUNKS)]
    while running:
        still = []
        for item in running:
            try:
                next(item)
                still.append(item)
            except StopIteration:
                pass
        running = still
    for copy in exchange:
        copy.wait_send()


def per_device(prior, terminal, perturbation, angles):
    n_space, n_mem = lax.axis_size("space"), lax.axis_size("mem")
    samples, variables = terminal.shape
    members = prior.shape[0] * n_mem
    nx = n_space // CORES
    ny = math.gcd(nx, n_mem)
    nz = n_mem // ny
    nxy = nx * ny
    rows = samples // CHUNKS
    rows2 = rows // CORES
    rows3 = rows2 // nxy
    scatter_z = rows3 % (nz * SUBLANES) == 0
    rows4 = rows3 // nz if scatter_z else rows3
    temper = math.sqrt(variables * n_space * n_mem)
    f32 = jnp.float32
    exchanges = 2 * (1 + nxy - 1 + nz - 1)
    iters = perturbation.shape[0]
    anywhere = pl.BlockSpec(memory_space=pl.ANY)
    return pl.pallas_call(
        functools.partial(kernel, (n_space, n_mem, ny, nz, scatter_z, temper)),
        out_shape=jax.ShapeDtypeStruct((samples, variables), f32),
        in_specs=[anywhere] * 3 + [pl.BlockSpec(memory_space=pltpu.VMEM)],
        out_specs=anywhere,
        scratch_shapes=[
            pltpu.VMEM((members, variables), f32),
            pltpu.VMEM((samples, variables), f32),
            pltpu.VMEM((iters, samples, variables), f32),
            pltpu.VMEM((CHUNKS, rows2, members), f32),
            pltpu.VMEM((CHUNKS, rows2, members), f32),
            pltpu.VMEM((CHUNKS, rows2, members), f32),
            pltpu.VMEM((CHUNKS, nxy - 1, rows3, members), f32),
            pltpu.VMEM((CHUNKS, rows3, members), f32),
            pltpu.VMEM((2, CHUNKS, nz - 1, rows4, members), f32),
            pltpu.VMEM((CHUNKS, rows, members), f32),
            pltpu.SemaphoreType.DMA((2, CHUNKS, exchanges)),
            pltpu.SemaphoreType.DMA((2, CHUNKS, exchanges)),
            pltpu.SemaphoreType.DMA((n_mem - 1,)),
            pltpu.SemaphoreType.DMA((n_mem - 1,)),
            pltpu.SemaphoreType.DMA((3,)),
            pltpu.SemaphoreType.DMA((CHUNKS,)),
        ],
        compiler_params=pltpu.CompilerParams(collective_id=0, has_side_effects=True),
    )(prior, terminal, perturbation, angles.reshape(1, variables))


def solution(mesh):
    in_specs = (
        P("mem", "space"),
        P(None, ("space", "mem")),
        P(None, None, ("space", "mem")),
        P(("space", "mem")),
    )
    out_specs = P(None, ("space", "mem"))
    return jax.shard_map(
        per_device, mesh=mesh, in_specs=in_specs, out_specs=out_specs, check_vma=False
    )
```

time: 457 us -> 96.1 us (0.21)
  waiting for transfers between devices: 362 us -> 0 us
  Pallas kernels: 10.9 us -> 94.1 us
  blocking collectives: 47.3 us -> 0 us
  between operations: 13.8 us -> 0.01 us
  other arithmetic: 12.8 us -> 0 us
  matrix products: 8.05 us -> 0 us
    psum x3 -> x0, waiting for transfers between devices: 362 us -> none  [per_device(): inner_pairing_matrix = lax.psum(partial_gram, ('space', 'mem'))]
    pallas_call x0 -> x1, Pallas kernels: none -> 94.1 us  [per_device(): pl.pallas_call(functools.partial(kernel, (n_space, n_mem, ny, nz, scatter...]
    all_to_all x1 -> x0, blocking collectives: 21.6 us -> none  [per_device(): lax.all_to_all(prior_ensemble, 'mem', split_axis=1, concat_axis=0, tiled=...]
    unnamed x1 -> x0, blocking collectives: 20 us -> none
    unnamed x3 -> x0, Pallas kernels: 10.9 us -> none
    dot_general x3 -> x0, matrix products: 8.05 us -> none  [per_device(): jnp.einsum('sv,mv->sm', gaussian_variates, particle_vectors, precision=pe...]
    div x3 -> x0, other arithmetic: 7.18 us -> none  [member_weights(): (2.0 * alpha * inner_pairing_matrix - alpha * alpha * particle_lengths[No...]
    psum x1 -> x0, blocking collectives: 5.68 us -> none  [per_device(): summed = lax.psum(local_norms, 'space')]
  transfers between devices with their start and end apart: 3 -> 0, of which waited for: 3 -> 0; matrix products, arithmetic and copies ran while one was open for 0% -> 0% of each run, Pallas kernels for 0% -> 0%
where the time goes in v1:
time: 96.1 us; the launch traced here: 95.9 us
  Pallas kernels  94.1 us (98%)
  local copies, waits for them, and re-layouts  1.87 us (2%)
    pallas_call x1, Pallas kernels, per_device(): pl.pallas_call(functools.partial(kernel, (n_space, n_mem, ny, nz, scatter...  94.1 us

profile of v1, /device:TPU:0, one launch (start us, length us, event | category | flops | bytes accessed | tf_op | source)
XLA Modules:
  0.0 95.9 jit_solution(10311154660354389046)
XLA Ops:
  0.0 94.1 %shard_map.46 = f32[512,256]{1,0:T(8,128)} custom-call(f32[64,2048]{1,0:T(8,128)} %prior.1, f32[512,256]{1,0:T(8,128)} %terminal.1, f32[3,512,256]{2,1,0:T(8,128)} %perturbation.1, f32[1,256]{1,0:T(1,128)} %bitcast.1), custom_call_target="tpu_custom_call" | custom-call | tf_op jit(solution)/shard_map/pallas_call | solution.py:294
  94.1 1.9 %copy.6 = f32[512,256]{1,0:T(8,128)} copy(f32[512,256]{1,0:T(8,128)} %shard_map.46) | data formatting | bytes 1048576

commit v2 on v1

v2 whole, which is shorter than its diff:
```python
import functools
import math

import jax
import jax.numpy as jnp
from jax import lax
from jax.experimental import pallas as pl
from jax.experimental.pallas import tpu as pltpu
from jax.sharding import PartitionSpec as P

ITERS = 3
CHUNKS = 4
CORES = 2
SUBLANES = 8
LANES = 128
MESH = pl.DeviceIdType.MESH
HIGHEST = lax.Precision.HIGHEST


def dot(a, b, contract_b):
    return lax.dot_general(
        a,
        b,
        (((1,), (contract_b,)), ((), ())),
        precision=HIGHEST,
        preferred_element_type=jnp.float32,
    )


def arctan(x):
    a = jnp.abs(x)
    big = a > 2.414213562373095
    mid = a > 0.4142135623730950
    num = jnp.where(big, -1.0, jnp.where(mid, a - 1.0, a))
    den = jnp.where(big, a, jnp.where(mid, a + 1.0, 1.0))
    base = jnp.where(big, math.pi / 2, jnp.where(mid, math.pi / 4, 0.0))
    r = num / den
    s = r * r
    poly = ((8.05374449538e-2 * s - 1.38776856032e-1) * s + 1.99777106478e-1) * s
    poly = (poly - 3.33329491539e-1) * s * r + r
    y = base + poly
    return jnp.where(x < 0.0, -y, y)


def rows_at(start, size):
    return pl.ds(pl.multiple_of(start, SUBLANES), size)


def kernel(
    plan,
    prior,
    terminal,
    perturbation,
    angles,
    out,
    x,
    z,
    noise,
    seen,
    gram,
    xy_in,
    part,
    z_in,
    numer,
    w,
    send,
    recv,
    once_send,
    once_recv,
    local,
):
    n_space, n_mem, ny, nz, scatter_z, temper = plan
    nxy = (n_space // CORES) * ny
    chunks, rows, _ = gram.shape
    rows3 = rows // nxy
    samples = z.shape[0]
    members = prior.shape[0]
    variables = terminal.shape[1]
    lanes = numer.shape[3]

    sp = lax.axis_index("space")
    me = lax.axis_index("mem")
    core = lax.rem(sp, CORES)
    other = 1 - core
    xi = lax.div(sp, CORES)
    yi = lax.rem(me, ny)
    zi = lax.div(me, ny)
    q = xi * ny + yi

    core_dev = (xi * CORES + other, me)

    def xy_peer(d):
        p = lax.rem(q + d, nxy)
        return p, (lax.div(p, ny) * CORES + core, zi * ny + lax.rem(p, ny))

    def z_peer(d):
        p = lax.rem(zi + d, nz)
        return p, (sp, p * ny + yi)

    def mem_peer(d):
        p = lax.rem(me + d, n_mem)
        return p, (sp, p)

    def cols(p):
        return pl.ds(pl.multiple_of(p * variables, variables), variables)

    mine = cols(core)
    my_samples = rows_at(core * samples, samples)
    its_samples = rows_at(other * samples, samples)
    my_members = rows_at(me * members, members)

    loads = [
        pltpu.make_async_copy(
            prior.at[:, cols(me)], x.at[my_members, mine], local.at[0]
        ),
        pltpu.make_async_copy(terminal.at[my_samples, :], z.at[:, mine], local.at[1]),
        pltpu.make_async_copy(angles, seen.at[:, mine], local.at[2]),
        pltpu.make_async_copy(
            perturbation.at[:, my_samples, :], noise.at[:, :, mine], local.at[3]
        ),
    ]
    for copy in loads:
        copy.start()

    barrier = pltpu.get_barrier_semaphore()
    greet = [core_dev]
    greet += [xy_peer(d)[1] for d in range(1, nxy)]
    greet += [mem_peer(d)[1] for d in range(1, n_mem)]
    for dev in greet:
        pl.semaphore_signal(barrier, inc=1, device_id=dev, device_id_type=MESH)
    pl.semaphore_wait(barrier, len(greet))

    def put_once(src, dst, i, dev):
        copy = pltpu.make_async_remote_copy(
            src_ref=src,
            dst_ref=dst,
            send_sem=once_send.at[i],
            recv_sem=once_recv.at[i],
            device_id=dev,
            device_id_type=MESH,
        )
        copy.start()
        return copy

    exchange = []
    for d in range(1, n_mem):
        p, dev = mem_peer(d)
        exchange.append(put_once(prior.at[:, cols(p)], x.at[my_members, mine], d - 1, dev))
    i = n_mem - 1
    swaps = [
        put_once(terminal.at[its_samples, :], z.at[:, mine], i, core_dev),
        put_once(angles, seen.at[:, mine], i + 1, core_dev),
        put_once(prior.at[:, cols(me)], x.at[my_members, mine], i + 2, core_dev),
        put_once(perturbation.at[:, its_samples, :], noise.at[:, :, mine], i + 3, core_dev),
    ]
    i = i + 4
    for d, copy in enumerate(exchange):
        copy.wait_recv()
        theirs = rows_at(lax.rem(me + n_mem - d - 1, n_mem) * members, members)
        swaps.append(put_once(x.at[theirs, mine], x.at[theirs, mine], i + d, core_dev))
    i = i + n_mem - 1
    for copy in loads:
        copy.wait()
    for copy in swaps:
        copy.wait_recv()

    xs = x[...]
    norms = dot(jnp.ones((SUBLANES, xs.shape[1]), jnp.float32), xs * xs, 1)[:1]

    first_z = nxy - 1
    first_gz = first_z + nz - 1
    first_gxy = first_gz + nz - 1

    def chunk(c):
        where = pl.ds(c * rows, rows)
        mine_xy = rows_at(q * rows3, rows3)
        for k in range(ITERS):
            t = 1.0 - k / ITERS
            dt = 1.0 / ITERS
            alpha = 1.0 - 0.5 * t
            drift = -0.5 / alpha
            g2 = 1.0 + t / alpha
            damp = 1.0 - t
            started = []

            def put(src, dst, i, dev):
                copy = pltpu.make_async_remote_copy(
                    src_ref=src,
                    dst_ref=dst,
                    send_sem=send.at[k % 2, c, i],
                    recv_sem=recv.at[k % 2, c, i],
                    device_id=dev,
                    device_id_type=MESH,
                )
                copy.start()
                started.append(copy)
                return copy

            gram[c] = 2.0 * alpha * dot(z[where, :], x[...], 1) - alpha * alpha * norms
            group = []
            for d in range(1, nxy):
                p, dev = xy_peer(d)
                group.append(
                    put(gram.at[c, rows_at(p * rows3, rows3), :], xy_in.at[c, d - 1], d - 1, dev)
                )
            yield
            total = gram[c, mine_xy, :]
            for d, copy in enumerate(group):
                copy.wait_recv()
                total = total + xy_in[c, d]
            group = []
            if scatter_z:
                for p in range(nz):
                    part[c, p] = total[:, p * lanes : (p + 1) * lanes]
            else:
                part[c, 0] = total
            for d in range(1, nz):
                p, dev = z_peer(d)
                src = part.at[c, p] if scatter_z else part.at[c, 0]
                group.append(put(src, z_in.at[k % 2, c, d - 1], first_z + d - 1, dev))
            yield
            block = part[c, zi] if scatter_z else part[c, 0]
            for d, copy in enumerate(group):
                copy.wait_recv()
                block = block + z_in[k % 2, c, d]
            if scatter_z:
                numer[c, zi] = block
                group = [
                    put(numer.at[c, zi], numer.at[c, zi], first_gz + d - 1, z_peer(d)[1])
                    for d in range(1, nz)
                ]
                yield
                for copy in group:
                    copy.wait_recv()
                block = jnp.concatenate([numer[c, p] for p in range(nz)], axis=1)
            logits = block / (2.0 * t * temper)
            e = jnp.exp(logits - jnp.max(logits, axis=1, keepdims=True))
            w[c, mine_xy, :] = e / jnp.sum(e, axis=1, keepdims=True)
            group = [
                put(w.at[c, mine_xy, :], w.at[c, mine_xy, :], first_gxy + d - 1, xy_peer(d)[1])
                for d in range(1, nxy)
            ]
            yield
            for copy in group:
                copy.wait_recv()
            blend = dot(w[c], x[...], 0)
            zs = z[where, :]
            score = -(zs - alpha * blend) / t + damp * 4.0 * (seen[...] - arctan(zs)) / (
                1.0 + zs * zs
            )
            z[where, :] = (
                zs + dt * (-drift * zs + g2 * score) + math.sqrt(dt * g2) * noise[k, where, :]
            )
            for copy in started:
                copy.wait_send()
        target = out.at[rows_at(core * samples + c * rows, rows), :]
        result = pltpu.make_async_copy(z.at[where, mine], target, local.at[4 + c])
        result.start()
        swap = put_once(z.at[where, cols(other)], target, i + c, core_dev)
        yield
        result.wait()
        swap.wait()

    running = [chunk(c) for c in range(chunks)]
    while running:
        still = []
        for item in running:
            try:
                next(item)
                still.append(item)
            except StopIteration:
                pass
        running = still
    for copy in exchange + swaps:
        copy.wait_send()


def per_device(prior, terminal, perturbation, angles):
    n_space, n_mem = lax.axis_size("space"), lax.axis_size("mem")
    samples, variables = terminal.shape
    members = prior.shape[0] * n_mem
    nx = n_space // CORES
    ny = math.gcd(nx, n_mem)
    nz = n_mem // ny
    nxy = nx * ny
    half = samples // CORES
    chunks = CHUNKS
    while chunks > 1 and half % (chunks * nxy * SUBLANES):
        chunks //= 2
    rows = half // chunks
    rows3 = rows // nxy
    scatter_z = members % (nz * LANES) == 0
    pieces = nz if scatter_z else 1
    lanes = members // pieces
    temper = math.sqrt(variables * n_space * n_mem)
    f32 = jnp.float32
    exchanges = 2 * (nxy - 1 + nz - 1)
    once = 2 * (n_mem - 1) + 4 + chunks
    iters = perturbation.shape[0]
    anywhere = pl.BlockSpec(memory_space=pl.ANY)
    return pl.pallas_call(
        functools.partial(kernel, (n_space, n_mem, ny, nz, scatter_z, temper)),
        out_shape=jax.ShapeDtypeStruct((samples, variables), f32),
        in_specs=[anywhere] * 4,
        out_specs=anywhere,
        scratch_shapes=[
            pltpu.VMEM((members, CORES * variables), f32),
            pltpu.VMEM((half, CORES * variables), f32),
            pltpu.VMEM((iters, half, CORES * variables), f32),
            pltpu.VMEM((1, CORES * variables), f32),
            pltpu.VMEM((chunks, rows, members), f32),
            pltpu.VMEM((chunks, nxy - 1, rows3, members), f32),
            pltpu.VMEM((chunks, pieces, rows3, lanes), f32),
            pltpu.VMEM((2, chunks, nz - 1, rows3, lanes), f32),
            pltpu.VMEM((chunks, pieces, rows3, lanes), f32),
            pltpu.VMEM((chunks, rows, members), f32),
            pltpu.SemaphoreType.DMA((2, chunks, exchanges)),
            pltpu.SemaphoreType.DMA((2, chunks, exchanges)),
            pltpu.SemaphoreType.DMA((once,)),
            pltpu.SemaphoreType.DMA((once,)),
            pltpu.SemaphoreType.DMA((4 + chunks,)),
        ],
        compiler_params=pltpu.CompilerParams(collective_id=0, has_side_effects=True),
    )(prior, terminal, perturbation, angles.reshape(1, variables))


def solution(mesh):
    in_specs = (
        P("mem", "space"),
        P(None, ("space", "mem")),
        P(None, None, ("space", "mem")),
        P(("space", "mem")),
    )
    out_specs = P(None, ("space", "mem"))
    return jax.shard_map(
        per_device, mesh=mesh, in_specs=in_specs, out_specs=out_specs, check_vma=False
    )
```

time: 96.1 us -> 85.6 us (0.89)
  Pallas kernels: 94.1 us -> 83.6 us
    pallas_call x1, Pallas kernels: 94.1 us -> 83.6 us  [per_device(): pl.pallas_call(functools.partial(kernel, (n_space, n_mem, ny, nz, scatter...]
where the time goes in v2:
time: 85.6 us; the launch traced here: 85.5 us
  Pallas kernels  83.6 us (98%)
  local copies, waits for them, and re-layouts  1.87 us (2%)
    pallas_call x1, Pallas kernels, per_device(): pl.pallas_call(functools.partial(kernel, (n_space, n_mem, ny, nz, scatter...  83.6 us
    unnamed x1, local copies, waits for them, and re-layouts  1.87 us

profile of v2, /device:TPU:0, one launch (start us, length us, event | category | flops | bytes accessed | tf_op | source)
XLA Modules:
  0.0 85.5 jit_solution(16609091283149525990)
XLA Ops:
  0.0 83.6 %shard_map.46 = f32[512,256]{1,0:T(8,128)} custom-call(f32[64,2048]{1,0:T(8,128)} %prior.1, f32[512,256]{1,0:T(8,128)} %terminal.1, f32[3,512,256]{2,1,0:T(8,128)} %perturbation.1, f32[1,256]{1,0:T(1,128)} %bitcast.1), custom_call_target="tpu_custom_call" | custom-call | tf_op jit(solution)/shard_map/pallas_call | solution.py:301
  83.6 1.9 %copy.6 = f32[512,256]{1,0:T(8,128)} copy(f32[512,256]{1,0:T(8,128)} %shard_map.46) | data formatting | bytes 1048576

commit v3 on v2

--- a/solution.py
+++ b/solution.py
@@ -14,17 +14,32 @@
 SUBLANES = 8
 LANES = 128
 MESH = pl.DeviceIdType.MESH
-HIGHEST = lax.Precision.HIGHEST
-
-
-def dot(a, b, contract_b):
-    return lax.dot_general(
-        a,
-        b,
-        (((1,), (contract_b,)), ((), ())),
-        precision=HIGHEST,
-        preferred_element_type=jnp.float32,
-    )
+
+
+def split(a, parts):
+    out = []
+    for _ in range(parts):
+        out.append(a.astype(jnp.bfloat16))
+        a = a - out[-1].astype(jnp.float32)
+    return out
+
+
+def product(a, parts, contract_b):
+    n = a.shape[0]
+    lhs = split(a, len(parts))
+    total = None
+    for i in reversed(range(len(parts))):
+        rows = lhs[: len(parts) - i]
+        both = lax.dot_general(
+            jnp.concatenate(rows, axis=0),
+            parts[i],
+            (((1,), (contract_b,)), ((), ())),
+            preferred_element_type=jnp.float32,
+        )
+        for j in reversed(range(len(rows))):
+            term = both[j * n : (j + 1) * n]
+            total = term if total is None else total + term
+    return total
 
 
 def arctan(x):
@@ -63,13 +78,14 @@
     z_in,
     numer,
     w,
+    xb,
     send,
     recv,
     once_send,
     once_recv,
     local,
 ):
-    n_space, n_mem, ny, nz, scatter_z, temper = plan
+    n_space, n_mem, ny, nz, scatter_z, mixed, temper = plan
     nxy = (n_space // CORES) * ny
     chunks, rows, _ = gram.shape
     rows3 = rows // nxy
@@ -85,17 +101,28 @@
     xi = lax.div(sp, CORES)
     yi = lax.rem(me, ny)
     zi = lax.div(me, ny)
-    q = xi * ny + yi
 
     core_dev = (xi * CORES + other, me)
 
-    def xy_peer(d):
-        p = lax.rem(q + d, nxy)
-        return p, (lax.div(p, ny) * CORES + core, zi * ny + lax.rem(p, ny))
-
-    def z_peer(d):
-        p = lax.rem(zi + d, nz)
-        return p, (sp, p * ny + yi)
+    nx = n_space // CORES
+    nlow = ny if mixed else nz
+    here = {"x": xi, "y": yi, "low": lax.rem(zi, nlow), "high": lax.div(zi, nlow)}
+    size = {"x": nx, "y": ny, "low": nlow, "high": nz // nlow}
+
+    def position(axes):
+        return here[axes[0]] * size[axes[1]] + here[axes[1]]
+
+    def peer(axes, d):
+        p = lax.rem(position(axes) + d, size[axes[0]] * size[axes[1]])
+        at = dict(here)
+        at[axes[0]] = lax.div(p, size[axes[1]])
+        at[axes[1]] = lax.rem(p, size[axes[1]])
+        return p, (at["x"] * CORES + core, (at["high"] * nlow + at["low"]) * ny + at["y"])
+
+    orders = [(("x", "y"), ("high", "low"))]
+    if mixed:
+        orders += [orders[0], (("x", "low"), ("high", "y")), (("y", "low"), ("high", "x"))]
+    orders = [orders[c % len(orders)] for c in range(chunks)]
 
     def mem_peer(d):
         p = lax.rem(me + d, n_mem)
@@ -124,7 +151,9 @@
 
     barrier = pltpu.get_barrier_semaphore()
     greet = [core_dev]
-    greet += [xy_peer(d)[1] for d in range(1, nxy)]
+    for axes in sorted({axes for order in orders for axes in order}):
+        n = size[axes[0]] * size[axes[1]]
+        greet += [peer(axes, d)[1] for d in range(1, n)]
     greet += [mem_peer(d)[1] for d in range(1, n_mem)]
     for dev in greet:
         pl.semaphore_signal(barrier, inc=1, device_id=dev, device_id_type=MESH)
@@ -165,7 +194,17 @@
         copy.wait_recv()
 
     xs = x[...]
-    norms = dot(jnp.ones((SUBLANES, xs.shape[1]), jnp.float32), xs * xs, 1)[:1]
+    for j, piece in enumerate(split(xs, 3)):
+        xb[j] = piece
+    norms = jnp.zeros((SUBLANES, xs.shape[0]), jnp.float32)
+    for piece in reversed(split(xs * xs, 3)):
+        norms = norms + lax.dot_general(
+            jnp.ones((SUBLANES, xs.shape[1]), jnp.bfloat16),
+            piece,
+            (((1,), (1,)), ((), ())),
+            preferred_element_type=jnp.float32,
+        )
+    norms = norms[:1]
 
     first_z = nxy - 1
     first_gz = first_z + nz - 1
@@ -173,7 +212,9 @@
 
     def chunk(c):
         where = pl.ds(c * rows, rows)
-        mine_xy = rows_at(q * rows3, rows3)
+        first, second = orders[c]
+        mine_xy = rows_at(position(first) * rows3, rows3)
+        z_at = position(second)
         for k in range(ITERS):
             t = 1.0 - k / ITERS
             dt = 1.0 / ITERS
@@ -196,10 +237,10 @@
                 started.append(copy)
                 return copy
 
-            gram[c] = 2.0 * alpha * dot(z[where, :], x[...], 1) - alpha * alpha * norms
+            gram[c] = 2.0 * alpha * product(z[where, :], [xb[0], xb[1], xb[2]], 1) - alpha * alpha * norms
             group = []
             for d in range(1, nxy):
-                p, dev = xy_peer(d)
+                p, dev = peer(first, d)
                 group.append(
                     put(gram.at[c, rows_at(p * rows3, rows3), :], xy_in.at[c, d - 1], d - 1, dev)
                 )
@@ -215,18 +256,18 @@
             else:
                 part[c, 0] = total
             for d in range(1, nz):
-                p, dev = z_peer(d)
+                p, dev = peer(second, d)
                 src = part.at[c, p] if scatter_z else part.at[c, 0]
                 group.append(put(src, z_in.at[k % 2, c, d - 1], first_z + d - 1, dev))
             yield
-            block = part[c, zi] if scatter_z else part[c, 0]
+            block = part[c, z_at] if scatter_z else part[c, 0]
             for d, copy in enumerate(group):
                 copy.wait_recv()
                 block = block + z_in[k % 2, c, d]
             if scatter_z:
-                numer[c, zi] = block
+                numer[c, z_at] = block
                 group = [
-                    put(numer.at[c, zi], numer.at[c, zi], first_gz + d - 1, z_peer(d)[1])
+                    put(numer.at[c, z_at], numer.at[c, z_at], first_gz + d - 1, peer(second, d)[1])
                     for d in range(1, nz)
                 ]
                 yield
@@ -237,13 +278,13 @@
             e = jnp.exp(logits - jnp.max(logits, axis=1, keepdims=True))
             w[c, mine_xy, :] = e / jnp.sum(e, axis=1, keepdims=True)
             group = [
-                put(w.at[c, mine_xy, :], w.at[c, mine_xy, :], first_gxy + d - 1, xy_peer(d)[1])
+                put(w.at[c, mine_xy, :], w.at[c, mine_xy, :], first_gxy + d - 1, peer(first, d)[1])
                 for d in range(1, nxy)
             ]
             yield
             for copy in group:
                 copy.wait_recv()
-            blend = dot(w[c], x[...], 0)
+            blend = product(w[c], [xb[0], xb[1]], 0)
             zs = z[where, :]
             score = -(zs - alpha * blend) / t + damp * 4.0 * (seen[...] - arctan(zs)) / (
                 1.0 + zs * zs
@@ -292,6 +333,7 @@
     scatter_z = members % (nz * LANES) == 0
     pieces = nz if scatter_z else 1
     lanes = members // pieces
+    mixed = chunks == CHUNKS and nx == ny and nz % ny == 0
     temper = math.sqrt(variables * n_space * n_mem)
     f32 = jnp.float32
     exchanges = 2 * (nxy - 1 + nz - 1)
@@ -299,7 +341,7 @@
     iters = perturbation.shape[0]
     anywhere = pl.BlockSpec(memory_space=pl.ANY)
     return pl.pallas_call(
-        functools.partial(kernel, (n_space, n_mem, ny, nz, scatter_z, temper)),
+        functools.partial(kernel, (n_space, n_mem, ny, nz, scatter_z, mixed, temper)),
         out_shape=jax.ShapeDtypeStruct((samples, variables), f32),
         in_specs=[anywhere] * 4,
         out_specs=anywhere,
@@ -314,6 +356,7 @@
             pltpu.VMEM((2, chunks, nz - 1, rows3, lanes), f32),
             pltpu.VMEM((chunks, pieces, rows3, lanes), f32),
             pltpu.VMEM((chunks, rows, members), f32),
+            pltpu.VMEM((3, members, CORES * variables), jnp.bfloat16),
             pltpu.SemaphoreType.DMA((2, chunks, exchanges)),
             pltpu.SemaphoreType.DMA((2, chunks, exchanges)),
             pltpu.SemaphoreType.DMA((once,)),

time: 85.6 us -> 79.5 us (0.929)
  Pallas kernels: 83.6 us -> 77.4 us
    pallas_call x1, Pallas kernels: 83.6 us -> 77.4 us  [per_device(): pl.pallas_call(functools.partial(kernel, (n_space, n_mem, ny, nz, scatter...]
where the time goes in v3:
time: 79.5 us; the launch traced here: 79.3 us
  Pallas kernels  77.4 us (97%)
  local copies, waits for them, and re-layouts  1.87 us (2%)
    pallas_call x1, Pallas kernels, per_device(): pl.pallas_call(functools.partial(kernel, (n_space, n_mem, ny, nz, scatter...  77.4 us
    unnamed x1, local copies, waits for them, and re-layouts  1.87 us

profile of v3, /device:TPU:0, one launch (start us, length us, event | category | flops | bytes accessed | tf_op | source)
XLA Modules:
  0.0 79.3 jit_solution(4943880451690571945)
XLA Ops:
  0.0 77.4 %shard_map.46 = f32[512,256]{1,0:T(8,128)} custom-call(f32[64,2048]{1,0:T(8,128)} %prior.1, f32[512,256]{1,0:T(8,128)} %terminal.1, f32[3,512,256]{2,1,0:T(8,128)} %perturbation.1, f32[1,256]{1,0:T(1,128)} %bitcast.1), custom_call_target="tpu_custom_call" | custom-call | tf_op jit(solution)/shard_map/pallas_call | solution.py:343
  77.5 1.9 %copy.6 = f32[512,256]{1,0:T(8,128)} copy(f32[512,256]{1,0:T(8,128)} %shard_map.46) | data formatting | bytes 1048576

commit v4 on v3

--- a/solution.py
+++ b/solution.py
@@ -104,10 +104,8 @@
 
     core_dev = (xi * CORES + other, me)
 
-    nx = n_space // CORES
-    nlow = ny if mixed else nz
-    here = {"x": xi, "y": yi, "low": lax.rem(zi, nlow), "high": lax.div(zi, nlow)}
-    size = {"x": nx, "y": ny, "low": nlow, "high": nz // nlow}
+    here = {"x": xi, "y": yi, "z": zi, "one": 0}
+    size = {"x": n_space // CORES, "y": ny, "z": nz, "one": 1}
 
     def position(axes):
         return here[axes[0]] * size[axes[1]] + here[axes[1]]
@@ -117,11 +115,11 @@
         at = dict(here)
         at[axes[0]] = lax.div(p, size[axes[1]])
         at[axes[1]] = lax.rem(p, size[axes[1]])
-        return p, (at["x"] * CORES + core, (at["high"] * nlow + at["low"]) * ny + at["y"])
-
-    orders = [(("x", "y"), ("high", "low"))]
+        return p, (at["x"] * CORES + core, at["z"] * ny + at["y"])
+
+    orders = [(("x", "y"), ("one", "z"))]
     if mixed:
-        orders += [orders[0], (("x", "low"), ("high", "y")), (("y", "low"), ("high", "x"))]
+        orders += [orders[0][::-1], orders[0], orders[0]]
     orders = [orders[c % len(orders)] for c in range(chunks)]
 
     def mem_peer(d):
@@ -333,7 +331,7 @@
     scatter_z = members % (nz * LANES) == 0
     pieces = nz if scatter_z else 1
     lanes = members // pieces
-    mixed = chunks == CHUNKS and nx == ny and nz % ny == 0
+    mixed = nxy == nz and scatter_z
     temper = math.sqrt(variables * n_space * n_mem)
     f32 = jnp.float32
     exchanges = 2 * (nxy - 1 + nz - 1)

time: 79.5 us -> 77.3 us (0.972)
  Pallas kernels: 77.4 us -> 75.3 us
    pallas_call x1, Pallas kernels: 77.4 us -> 75.3 us  [per_device(): pl.pallas_call(functools.partial(kernel, (n_space, n_mem, ny, nz, scatter...]
where the time goes in v4:
time: 77.3 us; the launch traced here: 77.1 us
  Pallas kernels  75.3 us (97%)
  local copies, waits for them, and re-layouts  1.87 us (2%)
    pallas_call x1, Pallas kernels, per_device(): pl.pallas_call(functools.partial(kernel, (n_space, n_mem, ny, nz, scatter...  75.3 us
    unnamed x1, local copies, waits for them, and re-layouts  1.87 us

profile of v4, /device:TPU:0, one launch (start us, length us, event | category | flops | bytes accessed | tf_op | source)
XLA Modules:
  0.0 77.1 jit_solution(13203608879034148212)
XLA Ops:
  0.0 75.3 %shard_map.46 = f32[512,256]{1,0:T(8,128)} custom-call(f32[64,2048]{1,0:T(8,128)} %prior.1, f32[512,256]{1,0:T(8,128)} %terminal.1, f32[3,512,256]{2,1,0:T(8,128)} %perturbation.1, f32[1,256]{1,0:T(1,128)} %bitcast.1), custom_call_target="tpu_custom_call" | custom-call | tf_op jit(solution)/shard_map/pallas_call | solution.py:341
  75.3 1.9 %copy.6 = f32[512,256]{1,0:T(8,128)} copy(f32[512,256]{1,0:T(8,128)} %shard_map.46) | data formatting | bytes 1048576
